TPU v7x, 512 devices: a whole 4x8x8 slice. The times are simulated.
512 devices in a mesh: fsdp: 32 (over z, y_lo, core), dp: 4 (over y_hi), tensor: 4 (over x).
Axes of the slice: x: 4, y: 8 (y_hi: 4, y_lo: 2; y = y_hi * 2 + y_lo), z: 8, core: 2. Of those that a mesh axis runs over, the one named last changes fastest.
Arguments:
- master_weight: float32 [4096, 14336], P(('fsdp', 'dp'), 'tensor'), may hold values from -0.09375 to 0.09375
- first_moment: bfloat16 [4096, 14336], P(('fsdp', 'dp'), 'tensor'), may hold values from -6 to 6
- second_moment: bfloat16 [4096, 14336], P(('fsdp', 'dp'), 'tensor'), may hold values from 0.25 to 16
- teacher_weight: float32 [4096, 14336], P(('fsdp', 'dp'), 'tensor'), may hold values from -0.09375 to 0.09375
- grad_parts: bfloat16 [4, 4096, 14336], P('dp', 'fsdp', 'tensor'), may hold values from -6 to 6
- embed_table: bfloat16 [4096, 64128], P(('fsdp', 'dp', 'tensor')), may hold values from -6 to 6
- token_ids: int32 [32, 256], P('fsdp'), may hold values from 0 to 64127
- pair_ids: int32 [32, 256], P('fsdp'), may hold values from 0 to 7, never falling along the last dimension, each value on 1 to 64 neighbouring positions
- class_head: bfloat16 [4, 3584, 256], P('tensor', 'dp'), may hold values from -0.046875 to 0.046875
Outputs:
- master_new: float32 [4096, 14336], P(('fsdp', 'dp'), 'tensor')
- first_new: bfloat16 [4096, 14336], P(('fsdp', 'dp'), 'tensor')
- second_new: bfloat16 [4096, 14336], P(('fsdp', 'dp'), 'tensor')
- teacher_new: float32 [4096, 14336], P(('fsdp', 'dp'), 'tensor')
- class_logits: float32 [32, 8, 256], P('fsdp')
Inputs may be any that keep to these rules, and one draw needn't show every extreme that they name: `pair_ids`: in every row the pair numbers never fall, and each of the 8 pairs holds 1 to 64 tokens, one of them exactly 64.
All inputs are finite; a program needn't handle non-finite values.
Results may differ from a plain program's by a relative error of at most 0.0055.
Values may be sent and summed in bfloat16 or wider, within the bound.
No kernel may reach another device: no remote copies, remote signals or barrier semaphores. Data moves between devices by JAX's collectives and lax.ppermute only.
A program may use at most 128 MiB of HBM per device.

v0:
```python
import jax
import jax.numpy as jnp
from jax import lax
from jax.sharding import PartitionSpec as P

PAIRS = 8
beta_one = 0.9
beta_two = 0.95
learn_rate = 0.001
decay_rate = 0.1
ema_keep = 0.99


def optimizer_step(master_weight, first_moment, second_moment, teacher_weight, grad_parts):
    gradient = lax.psum_scatter(grad_parts[0], "dp", scatter_dimension=0, tiled=True).astype(
        jnp.float32
    )
    first_full = beta_one * first_moment.astype(jnp.float32) + (1.0 - beta_one) * gradient
    second_full = (
        beta_two * second_moment.astype(jnp.float32) + (1.0 - beta_two) * gradient * gradient
    )
    master_new = master_weight - learn_rate * (
        first_full / (jnp.sqrt(second_full) + 1e-08) + decay_rate * master_weight
    )
    teacher_new = ema_keep * teacher_weight + (1.0 - ema_keep) * master_new
    return (
        master_new,
        first_full.astype(jnp.bfloat16),
        second_full.astype(jnp.bfloat16),
        teacher_new,
    )


def ring_gather(block, axis):
    count = lax.axis_size(axis)
    right = [(i, (i + 1) % count) for i in range(count)]
    left = [(i, (i - 1) % count) for i in range(count)]
    place = lax.axis_index(axis)
    half = block.shape[0] // 2
    whole = jnp.zeros((count,) + block.shape, block.dtype)
    whole = lax.dynamic_update_index_in_dim(whole, block, place, 0)
    going_right = going_left = block
    for step in range(1, count // 2):
        going_right = lax.ppermute(going_right, axis, right)
        going_left = lax.ppermute(going_left, axis, left)
        whole = lax.dynamic_update_index_in_dim(whole, going_right, (place - step) % count, 0)
        whole = lax.dynamic_update_index_in_dim(whole, going_left, (place + step) % count, 0)
    first = lax.ppermute(going_right[:half], axis, right)
    second = lax.ppermute(going_left[half:], axis, left)
    last = jnp.concatenate([first, second], axis=0)
    return lax.dynamic_update_index_in_dim(whole, last, (place + count // 2) % count, 0)


def embed_inputs(embed_table, token_ids):
    every_id = lax.all_to_all(
        jnp.broadcast_to(token_ids, (32, token_ids.shape[1])), "fsdp", 0, 0, tiled=True
    )
    picked = embed_table.at[:, every_id.reshape(-1)].get(mode="promise_in_bounds")
    received = lax.all_to_all(
        picked.reshape(8, 32, 256).transpose(1, 0, 2),
        "fsdp",
        split_axis=0,
        concat_axis=0,
        tiled=True,
    )
    part = lax.all_gather(received.reshape(256, 256), "dp", axis=0, tiled=True)
    return ring_gather(part, "tensor")


def label_tokens(teacher_new, stacked, group_pairs, class_head):
    teacher_half = teacher_new.astype(jnp.bfloat16)
    replica_count = lax.axis_size("dp")
    rows = teacher_half.shape[0]
    width = teacher_half.shape[1] // replica_count
    split = teacher_half.reshape(rows, replica_count, width).transpose(1, 0, 2)
    block = lax.all_to_all(split.reshape(-1, width), "dp", 0, 0, tiled=True)
    row_block = lax.all_gather(block, "fsdp", axis=0, tiled=True)
    inputs = stacked.reshape(4, 4, 32, 8, 256).transpose(2, 1, 0, 3, 4).reshape(4096, 256)
    values = inputs.astype(jnp.float32)
    scale = lax.rsqrt(jnp.mean(values * values, axis=0, keepdims=True) + 1e-05)
    normed = (values * scale).astype(jnp.bfloat16)
    hidden = jnp.einsum("fk,fo->ko", normed, row_block, preferred_element_type=jnp.float32)
    group_count = group_pairs.shape[0]
    active = jax.nn.silu(hidden).reshape(group_count, -1, width)
    member_of = (
        group_pairs[:, None, :] == jnp.arange(PAIRS, dtype=jnp.int32)[None, :, None]
    ).astype(jnp.float32)
    totals = jnp.einsum("gpt,gtk->gpk", member_of, active, precision=lax.Precision.HIGHEST)
    pooled = (totals / jnp.sum(member_of, axis=2, keepdims=True)).astype(jnp.bfloat16)
    head_part = class_head[0]
    partial_terms = jnp.einsum("gpk,kc->gpc", pooled, head_part, preferred_element_type=jnp.float32)
    return lax.psum(lax.psum(partial_terms, "dp"), "tensor")


def shards(
    master_weight,
    first_moment,
    second_moment,
    teacher_weight,
    grad_parts,
    embed_table,
    token_ids,
    pair_ids,
    class_head,
):
    master_new, first_new, second_new, teacher_new = optimizer_step(
        master_weight, first_moment, second_moment, teacher_weight, grad_parts
    )
    stacked = embed_inputs(embed_table, token_ids)
    class_logits = label_tokens(teacher_new, stacked, pair_ids, class_head)
    return (master_new, first_new, second_new, teacher_new, class_logits)


def solution(mesh):
    placed = (
        P(("fsdp", "dp"), "tensor"),
        P(("fsdp", "dp"), "tensor"),
        P(("fsdp", "dp"), "tensor"),
        P(("fsdp", "dp"), "tensor"),
        P("dp", "fsdp", "tensor"),
        P(("fsdp", "dp", "tensor"), None),
        P("fsdp", None),
        P("fsdp", None),
        P("tensor", "dp", None),
    )
    return jax.shard_map(
        shards,
        mesh=mesh,
        in_specs=placed,
        out_specs=(
            P(("fsdp", "dp"), "tensor"),
            P(("fsdp", "dp"), "tensor"),
            P(("fsdp", "dp"), "tensor"),
            P(("fsdp", "dp"), "tensor"),
            P("fsdp", None, None),
        ),
        check_vma=False,
    )
```

profile of v0, /device:TPU:8, one launch (start us, length us, event | category | flops | bytes accessed | tf_op | source)
XLA Modules:
  0.0 217.0 jit_solution(6691346589471912774)
XLA Ops:
  7.2 0.7 reduce-scatter.2.cloned.1.call-update
  8.0 42.5 %reduce-scatter.2.cloned.1.call-done = bf16[32,3584]{1,0:T(8,128)(2,1)} async-done(((bf16[128,3584]{1,0:T(8,128)(2,1)}), bf16[32,3584]{1,0:T(8,128)(2,1)}) %reduce-scatter.2.cloned.1.call-update) | async-done | bytes 229392 | tf_op jit(solution)/shard_map/reduce_scatter | solution.py:15
  50.4 2.9 %fusion.16 = (bf16[32,3584]{1,0:T(8,128)(2,1)S(1)}, f32[32,3584]{1,0:T(8,128)}, f32[32,3584]{1,0:T(8,128)}, bf16[32,3584]{1,0:T(8,128)(2,1)}, bf16[32,3584]{1,0:T(8,128)(2,1)}) fusion(f32[32,3584]{1,0:T(8,128)} %param.12, f32[32,3584]{1,0:T(8,128)} %param.9, bf16[32,3584]{1,0:T(8,128)(2,1)} %param.11, bf16[32,3584]{1,0:T(8,128)(2,1)} %reduce-scatter.2.cloned.1.call-done, ...), kind=kLoop, calls=%fused_computation.35 | loop fusion | flops 2523136 | bytes 3211264 | tf_op jit(solution)/shard_map/convert_element_type | solution.py:71
  53.5 14.2 %all_to_all.20 = bf16[4,32,896]{2,1,0:T(8,128)(2,1)} all-to-all(bf16[4,32,896]{2,1,0:T(8,128)(2,1)S(1)} %copy.28), channel_id=1, replica_groups=mesh['fsdp'=32,'dp'=4,'tensor'=4] {'dp'}, dimensions={0} | all-to-all | bytes 458752 | tf_op jit(solution)/shard_map/all_to_all | solution.py:76
  67.7 0.6 broadcast_in_dim.27
  68.3 8.6 %all-to-all-start = ((s32[32,1,256]{2,1,0:T(1,128)}), s32[32,1,256]{2,1,0:T(1,128)S(1)}, u32[]{:S(2)}, u32[]{:S(2)}) async-start(s32[32,1,256]{2,1,0:T(1,128)} %broadcast_in_dim.27), calls=%async_computation.1 | async-start | bytes 65536 | tf_op jit(solution)/shard_map/all_to_all | solution.py:55
  76.9 10.7 %copy.25 = bf16[8,64128]{0,1:T(8,128)(2,1)} copy(bf16[8,64128]{1,0:T(8,128)(2,1)S(1)} %copy-done.1) | data formatting | bytes 2052096 | tf_op args[5]
  87.6 29.9 %gather_fusion = bf16[8192,8]{1,0:T(8,128)(2,1)S(1)} fusion(bf16[8,64128]{0,1:T(8,128)(2,1)} %copy.25, s32[8192]{0:T(1024)S(1)} %broadcast_clamp_fusion), kind=kCustom, calls=%fused_computation | custom fusion | bytes 294912 | tf_op jit(solution)/shard_map/gather | solution.py:58
  117.6 0.8 copy.26
  118.3 17.7 %all_to_all.21 = bf16[32,8,256]{2,1,0:T(8,128)(2,1)S(1)} all-to-all(bf16[32,8,256]{2,1,0:T(8,128)(2,1)S(1)} %bitcast.42), channel_id=1, replica_groups=mesh['fsdp'=32,'dp'=4,'tensor'=4] {'fsdp'}, dimensions={0} | all-to-all | bytes 262144 | tf_op jit(solution)/shard_map/all_to_all | solution.py:59
  136.0 16.4 %all_gather.6 = bf16[1024,256]{1,0:T(8,128)(2,1)S(1)} all-gather(bf16[256,256]{1,0:T(8,128)(2,1)S(1)} %bitcast.43), channel_id=1, replica_groups=mesh['fsdp'=32,'dp'=4,'tensor'=4] {'dp'}, dimensions={0}, use_global_device_ids=true | all-gather | bytes 655360 | tf_op jit(solution)/shard_map/all_gather | solution.py:66
  152.4 3.2 %collective-permute-start = (bf16[1024,256]{1,0:T(8,128)(2,1)S(1)}, bf16[1024,256]{1,0:T(8,128)(2,1)S(1)}, u32[]{:S(2)}, u32[]{:S(2)}) collective-permute-start(bf16[1024,256]{1,0:T(8,128)(2,1)S(1)} %all_gather.6), channel_id=1, source_target_pairs={{0,1},{1,2},{2,3},{3,0},{4,5},{5,6},{6,7},{7,4},{8,9},{9,10},{10,1... | collective-permute-start | bytes 1572872 | tf_op jit(solution)/shard_map/ppermute | solution.py:44
  155.6 3.8 %collective-permute-start.1 = (bf16[1024,256]{1,0:T(8,128)(2,1)S(1)}, bf16[1024,256]{1,0:T(8,128)(2,1)S(1)}, u32[]{:S(2)}, u32[]{:S(2)}) collective-permute-start(bf16[1024,256]{1,0:T(8,128)(2,1)S(1)} %all_gather.6), channel_id=1, source_target_pairs={{0,3},{1,0},{2,1},{3,2},{4,7},{5,4},{6,5},{7,6},{8,11},{9,8},{10,9... | collective-permute-start | bytes 1572872 | tf_op jit(solution)/shard_map/ppermute | solution.py:45
  159.8 6.1 %collective-permute-done = bf16[1024,256]{1,0:T(8,128)(2,1)S(1)} collective-permute-done((bf16[1024,256]{1,0:T(8,128)(2,1)S(1)}, bf16[1024,256]{1,0:T(8,128)(2,1)S(1)}, u32[]{:S(2)}, u32[]{:S(2)}) %collective-permute-start) | collective-permute-done | bytes 524320 | tf_op jit(solution)/shard_map/ppermute | solution.py:44
  166.0 2.3 %collective-permute-start.2 = (bf16[512,256]{1,0:T(8,128)(2,1)S(1)}, bf16[512,256]{1,0:T(8,128)(2,1)S(1)}, u32[]{:S(2)}, u32[]{:S(2)}) collective-permute-start(bf16[512,256]{1,0:T(8,128)(2,1)S(1)} %slice.10), channel_id=1, source_target_pairs={{0,1},{1,2},{2,3},{3,0},{4,5},{5,6},{6,7},{7,4},{8,9},{9,10},{10,1... | collective-permute-start | bytes 786440 | tf_op jit(solution)/shard_map/ppermute | solution.py:48
  168.3 4.8 %collective-permute-start.3 = (bf16[512,256]{1,0:T(8,128)(2,1)S(1)}, bf16[512,256]{1,0:T(8,128)(2,1)S(1)}, u32[]{:S(2)}, u32[]{:S(2)}) collective-permute-start(bf16[512,256]{1,0:T(8,128)(2,1)S(1)} %slice.11), channel_id=1, source_target_pairs={{0,3},{1,0},{2,1},{3,2},{4,7},{5,4},{6,5},{7,6},{8,11},{9,8},{10,9... | collective-permute-start | bytes 786440 | tf_op jit(solution)/shard_map/ppermute | solution.py:49
  173.2 2.3 %collective-permute-done.2 = bf16[512,256]{1,0:T(8,128)(2,1)S(1)} collective-permute-done((bf16[512,256]{1,0:T(8,128)(2,1)S(1)}, bf16[512,256]{1,0:T(8,128)(2,1)S(1)}, u32[]{:S(2)}, u32[]{:S(2)}) %collective-permute-start.2) | collective-permute-done | bytes 262176 | tf_op jit(solution)/shard_map/ppermute | solution.py:48
  175.4 1.5 collective-permute-done.3
  177.3 0.6 copy.27
  178.6 0.6 fusion
  179.2 5.5 %fusion.17 = f32[256,896]{1,0:T(8,128)S(1)} fusion(bf16[4096,256]{1,0:T(8,128)(2,1)S(1)} %fusion, bf16[4096,896]{1,0:T(8,128)(2,1)} %all-gather.2.cloned.1.call-done), kind=kOutput, calls=%fused_computation.36 | convolution fusion | flops 1879048192 | bytes 10354688 | tf_op jit(solution)/shard_map/fk,fo->ko/dot_general | solution.py:82
  184.7 0.6 fusion.1
  185.5 12.5 %psum.14 = f32[1,8,256]{2,1,0:T(8,128)S(1)} all-reduce(f32[1,8,256]{2,1,0:T(8,128)S(1)} %convolution_bitcast_fusion), channel_id=1, replica_groups=mesh['fsdp'=32,'dp'=4,'tensor'=4] {'dp'}, use_global_device_ids=true, to_apply=%region_3.4 | all-reduce | flops 2048 | bytes 16384 | tf_op jit(solution)/shard_map/psum | solution.py:92
  198.0 12.1 %psum.15 = f32[1,8,256]{2,1,0:T(8,128)} all-reduce(f32[1,8,256]{2,1,0:T(8,128)S(1)} %psum.14), channel_id=1, replica_groups=mesh['fsdp'=32,'dp'=4,'tensor'=4] {'tensor'}, use_global_device_ids=true, to_apply=%region_4.5 | all-reduce | flops 2048 | bytes 16384 | tf_op jit(solution)/shard_map/psum | solution.py:92
  (30 shorter events, 1.8 us)
Async XLA Ops:
  7.2 178.2 %copy-start = (bf16[1,896,256]{2,1,0:T(8,128)(2,1)S(1)}, bf16[1,896,256]{2,1,0:T(8,128)(2,1)}, u32[]{:S(2)}) copy-start(bf16[1,896,256]{2,1,0:T(8,128)(2,1)} %param.17) | copy-start | bytes 1376260
  7.2 43.3 %reduce-scatter.2.cloned.1.call-start = ((), (), s32[]{:S(2)}) async-start(), calls=%async_computation.4 | async-start | bytes 1146880 | tf_op jit(solution)/shard_map/reduce_scatter | solution.py:15
  7.9 59.7 %copy-start.2 = (s32[1,256]{1,0:T(1,128)S(1)}, s32[1,256]{1,0:T(1,128)}, u32[]{:S(2)}) copy-start(s32[1,256]{1,0:T(1,128)} %param.15) | copy-start | bytes 3076
  7.9 69.0 %copy-start.1 = (bf16[8,64128]{1,0:T(8,128)(2,1)S(1)}, bf16[8,64128]{1,0:T(8,128)(2,1)}, u32[]{:S(2)}) copy-start(bf16[8,64128]{1,0:T(8,128)(2,1)} %param.14) | copy-start | bytes 3078148
  7.9 171.3 %all-gather.2.cloned.1.call-start = ((), (), s32[]{:S(2)}) async-start(), calls=%async_computation.5 | async-start | bytes 7569408 | tf_op jit(solution)/shard_map/all_gather | solution.py:77
  68.3 19.3 %all-to-all-start = ((s32[32,1,256]{2,1,0:T(1,128)}), s32[32,1,256]{2,1,0:T(1,128)S(1)}, u32[]{:S(2)}, u32[]{:S(2)}) async-start(s32[32,1,256]{2,1,0:T(1,128)} %broadcast_in_dim.27), calls=%async_computation.1 | async-start | bytes 65536 | tf_op jit(solution)/shard_map/all_to_all | solution.py:55
  87.6 71.9 %copy-start.3 = (s32[1,256]{1,0:T(1,128)S(1)}, s32[1,256]{1,0:T(1,128)}, u32[]{:S(2)}) copy-start(s32[1,256]{1,0:T(1,128)} %param.16) | copy-start | bytes 3076
  152.4 13.5 %collective-permute-start = (bf16[1024,256]{1,0:T(8,128)(2,1)S(1)}, bf16[1024,256]{1,0:T(8,128)(2,1)S(1)}, u32[]{:S(2)}, u32[]{:S(2)}) collective-permute-start(bf16[1024,256]{1,0:T(8,128)(2,1)S(1)} %all_gather.6), channel_id=1, source_target_pairs={{0,1},{1,2},{2,3},{3,0},{4,5},{5,6},{6,7},{7,4},{8,9},{9,10},{10,1... | collective-permute-start | bytes 1572872 | tf_op jit(solution)/shard_map/ppermute | solution.py:44
  155.6 12.6 %collective-permute-start.1 = (bf16[1024,256]{1,0:T(8,128)(2,1)S(1)}, bf16[1024,256]{1,0:T(8,128)(2,1)S(1)}, u32[]{:S(2)}, u32[]{:S(2)}) collective-permute-start(bf16[1024,256]{1,0:T(8,128)(2,1)S(1)} %all_gather.6), channel_id=1, source_target_pairs={{0,3},{1,0},{2,1},{3,2},{4,7},{5,4},{6,5},{7,6},{8,11},{9,8},{10,9... | collective-permute-start | bytes 1572872 | tf_op jit(solution)/shard_map/ppermute | solution.py:45
  166.0 9.5 %collective-permute-start.2 = (bf16[512,256]{1,0:T(8,128)(2,1)S(1)}, bf16[512,256]{1,0:T(8,128)(2,1)S(1)}, u32[]{:S(2)}, u32[]{:S(2)}) collective-permute-start(bf16[512,256]{1,0:T(8,128)(2,1)S(1)} %slice.10), channel_id=1, source_target_pairs={{0,1},{1,2},{2,3},{3,0},{4,5},{5,6},{6,7},{7,4},{8,9},{9,10},{10,1... | collective-permute-start | bytes 786440 | tf_op jit(solution)/shard_map/ppermute | solution.py:48
  168.3 8.7 %collective-permute-start.3 = (bf16[512,256]{1,0:T(8,128)(2,1)S(1)}, bf16[512,256]{1,0:T(8,128)(2,1)S(1)}, u32[]{:S(2)}, u32[]{:S(2)}) collective-permute-start(bf16[512,256]{1,0:T(8,128)(2,1)S(1)} %slice.11), channel_id=1, source_target_pairs={{0,3},{1,0},{2,1},{3,2},{4,7},{5,4},{6,5},{7,6},{8,11},{9,8},{10,9... | collective-permute-start | bytes 786440 | tf_op jit(solution)/shard_map/ppermute | solution.py:49
Sparse Core Ops, SparseCore 0:
  10.8 39.5 reduce-scatter.1
  67.8 72.7 all-gather.1
where the time goes:
time: 217 us
  blocking collectives  72.8 us (34%)
  waiting for transfers between devices  53.1 us (24%)
  local copies, waits for them, and re-layouts  43 us (20%)
  starting transfers between devices  22.8 us (11%)
  between operations  14.3 us (7%)
  matrix products  6.27 us (3%)
  other arithmetic  4.68 us (2%)
    reduce_scatter x1, waiting for transfers between devices, optimizer_step(): lax.psum_scatter(grad_parts[0], 'dp', scatter_dimension=0, tiled=True)  42.5 us
    gather x1, local copies, waits for them, and re-layouts, embed_inputs(): embed_table.at[:, every_id.reshape(-1)].get(mode='promise_in_bounds')  29.9 us
    psum x2, blocking collectives, label_tokens(): return lax.psum(lax.psum(partial_terms, 'dp'), 'tensor')  24.6 us
    all_to_all x1, blocking collectives, embed_inputs(): lax.all_to_all(picked.reshape(8, 32, 256).transpose(1, 0, 2), 'fsdp', spl...  17.7 us
    all_gather x1, blocking collectives, embed_inputs(): part = lax.all_gather(received.reshape(256, 256), 'dp', axis=0, tiled=True)  16.4 us
    all_to_all x1, blocking collectives, label_tokens(): block = lax.all_to_all(split.reshape(-1, width), 'dp', 0, 0, tiled=True)  14.2 us
    unnamed x9, local copies, waits for them, and re-layouts  10.7 us
    all_to_all x1, starting transfers between devices, embed_inputs(): lax.all_to_all(jnp.broadcast_to(token_ids, (32, token_ids.shape[1])), 'fs...  8.59 us
  transfers between devices with their start and end apart: 7, of which 4 were waited for; matrix products, arithmetic and copies ran while one was open for 21% of the time, Pallas kernels for 0%

commit v1 on v0

--- a/solution.py
+++ b/solution.py
@@ -1,3 +1,4 @@
+import functools
 import jax
 import jax.numpy as jnp
 from jax import lax
@@ -9,6 +10,13 @@
 learn_rate = 0.001
 decay_rate = 0.1
 ema_keep = 0.99
+
+
+def form_slices(xin, chip_axis):
+    return lax.all_gather(xin, chip_axis).sum(axis=0)
+
+
+note_patch_over_axis = functools.partial(form_slices, chip_axis="tensor")
 
 
 def optimizer_step(master_weight, first_moment, second_moment, teacher_weight, grad_parts):
@@ -89,7 +97,7 @@
     pooled = (totals / jnp.sum(member_of, axis=2, keepdims=True)).astype(jnp.bfloat16)
     head_part = class_head[0]
     partial_terms = jnp.einsum("gpk,kc->gpc", pooled, head_part, preferred_element_type=jnp.float32)
-    return lax.psum(lax.psum(partial_terms, "dp"), "tensor")
+    return note_patch_over_axis(lax.psum(partial_terms, "dp"))
 
 
 def shards(

time: 217 us -> 219 us (level)
  the two profiles are of different devices: /device:TPU:8 before, /device:TPU:10 now
where the time goes in v1:
time: 219 us; the launch traced here: 218 us
  blocking collectives  74.4 us (34%)
  waiting for transfers between devices  54.3 us (25%)
  local copies, waits for them, and re-layouts  43 us (20%)
  starting transfers between devices  20.8 us (9%)
  between operations  14.3 us (7%)
  matrix products  6.27 us (3%)
  other arithmetic  5.28 us (2%)
    reduce_scatter x1, waiting for transfers between devices, optimizer_step(): lax.psum_scatter(grad_parts[0], 'dp', scatter_dimension=0, tiled=True)  41.4 us
    gather x1, local copies, waits for them, and re-layouts, embed_inputs(): embed_table.at[:, every_id.reshape(-1)].get(mode='promise_in_bounds')  29.9 us
    all_to_all x1, blocking collectives, embed_inputs(): lax.all_to_all(picked.reshape(8, 32, 256).transpose(1, 0, 2), 'fsdp', spl...  17.7 us
    all_gather x1, blocking collectives, embed_inputs(): part = lax.all_gather(received.reshape(256, 256), 'dp', axis=0, tiled=True)  16.2 us
    all_to_all x1, blocking collectives, label_tokens(): block = lax.all_to_all(split.reshape(-1, width), 'dp', 0, 0, tiled=True)  14.7 us
    all_gather x1, blocking collectives, form_slices(): return lax.all_gather(xin, chip_axis).sum(axis=0)  13.5 us
    psum x1, blocking collectives, label_tokens(): return note_patch_over_axis(lax.psum(partial_terms, 'dp'))  12.3 us
    unnamed x9, local copies, waits for them, and re-layouts  10.7 us
  transfers between devices with their start and end apart: 7, of which 4 were waited for; matrix products, arithmetic and copies ran while one was open for 20% of the time, Pallas kernels for 0%

profile of v1, /device:TPU:10, one launch (start us, length us, event | category | flops | bytes accessed | tf_op | source)
XLA Modules:
  0.0 218.4 jit_solution(6358296071925762459)
XLA Ops:
  7.2 0.7 reduce-scatter.2.cloned.1.call-update
  8.0 41.4 %reduce-scatter.2.cloned.1.call-done = bf16[32,3584]{1,0:T(8,128)(2,1)} async-done(((bf16[128,3584]{1,0:T(8,128)(2,1)}), bf16[32,3584]{1,0:T(8,128)(2,1)}) %reduce-scatter.2.cloned.1.call-update) | async-done | bytes 229392 | tf_op jit(solution)/shard_map/reduce_scatter | solution.py:23
  49.4 2.9 %fusion.16 = (bf16[32,3584]{1,0:T(8,128)(2,1)S(1)}, f32[32,3584]{1,0:T(8,128)}, f32[32,3584]{1,0:T(8,128)}, bf16[32,3584]{1,0:T(8,128)(2,1)}, bf16[32,3584]{1,0:T(8,128)(2,1)}) fusion(f32[32,3584]{1,0:T(8,128)} %param.12, f32[32,3584]{1,0:T(8,128)} %param.9, bf16[32,3584]{1,0:T(8,128)(2,1)} %param.11, bf16[32,3584]{1,0:T(8,128)(2,1)} %reduce-scatter.2.cloned.1.call-done, ...), kind=kLoop, calls=%fused_computation.35 | loop fusion | flops 2523136 | bytes 3211264 | tf_op jit(solution)/shard_map/convert_element_type | solution.py:79
  52.4 14.7 %all_to_all.20 = bf16[4,32,896]{2,1,0:T(8,128)(2,1)} all-to-all(bf16[4,32,896]{2,1,0:T(8,128)(2,1)S(1)} %copy.28), channel_id=1, replica_groups=mesh['fsdp'=32,'dp'=4,'tensor'=4] {'dp'}, dimensions={0} | all-to-all | bytes 458752 | tf_op jit(solution)/shard_map/all_to_all | solution.py:84
  67.2 0.6 broadcast_in_dim.27
  67.8 9.1 %all-to-all-start = ((s32[32,1,256]{2,1,0:T(1,128)}), s32[32,1,256]{2,1,0:T(1,128)S(1)}, u32[]{:S(2)}, u32[]{:S(2)}) async-start(s32[32,1,256]{2,1,0:T(1,128)} %broadcast_in_dim.27), calls=%async_computation.1 | async-start | bytes 65536 | tf_op jit(solution)/shard_map/all_to_all | solution.py:63
  76.9 10.7 %copy.25 = bf16[8,64128]{0,1:T(8,128)(2,1)} copy(bf16[8,64128]{1,0:T(8,128)(2,1)S(1)} %copy-done.1) | data formatting | bytes 2052096 | tf_op args[5]
  87.6 29.9 %gather_fusion = bf16[8192,8]{1,0:T(8,128)(2,1)S(1)} fusion(bf16[8,64128]{0,1:T(8,128)(2,1)} %copy.25, s32[8192]{0:T(1024)S(1)} %broadcast_clamp_fusion), kind=kCustom, calls=%fused_computation | custom fusion | bytes 294912 | tf_op jit(solution)/shard_map/gather | solution.py:66
  117.6 0.8 copy.26
  118.3 17.7 %all_to_all.21 = bf16[32,8,256]{2,1,0:T(8,128)(2,1)S(1)} all-to-all(bf16[32,8,256]{2,1,0:T(8,128)(2,1)S(1)} %bitcast.43), channel_id=1, replica_groups=mesh['fsdp'=32,'dp'=4,'tensor'=4] {'fsdp'}, dimensions={0} | all-to-all | bytes 262144 | tf_op jit(solution)/shard_map/all_to_all | solution.py:67
  136.0 16.2 %all_gather.12 = bf16[1024,256]{1,0:T(8,128)(2,1)S(1)} all-gather(bf16[256,256]{1,0:T(8,128)(2,1)S(1)} %bitcast.44), channel_id=1, replica_groups=mesh['fsdp'=32,'dp'=4,'tensor'=4] {'dp'}, dimensions={0}, use_global_device_ids=true | all-gather | bytes 655360 | tf_op jit(solution)/shard_map/all_gather | solution.py:74
  152.2 3.3 %collective-permute-start = (bf16[1024,256]{1,0:T(8,128)(2,1)S(1)}, bf16[1024,256]{1,0:T(8,128)(2,1)S(1)}, u32[]{:S(2)}, u32[]{:S(2)}) collective-permute-start(bf16[1024,256]{1,0:T(8,128)(2,1)S(1)} %all_gather.12), channel_id=1, source_target_pairs={{0,1},{1,2},{2,3},{3,0},{4,5},{5,6},{6,7},{7,4},{8,9},{9,10},{10,1... | collective-permute-start | bytes 1572872 | tf_op jit(solution)/shard_map/ppermute | solution.py:52
  155.5 2.5 %collective-permute-start.1 = (bf16[1024,256]{1,0:T(8,128)(2,1)S(1)}, bf16[1024,256]{1,0:T(8,128)(2,1)S(1)}, u32[]{:S(2)}, u32[]{:S(2)}) collective-permute-start(bf16[1024,256]{1,0:T(8,128)(2,1)S(1)} %all_gather.12), channel_id=1, source_target_pairs={{0,3},{1,0},{2,1},{3,2},{4,7},{5,4},{6,5},{7,6},{8,11},{9,8},{10,9... | collective-permute-start | bytes 1572872 | tf_op jit(solution)/shard_map/ppermute | solution.py:53
  158.4 6.4 %collective-permute-done = bf16[1024,256]{1,0:T(8,128)(2,1)S(1)} collective-permute-done((bf16[1024,256]{1,0:T(8,128)(2,1)S(1)}, bf16[1024,256]{1,0:T(8,128)(2,1)S(1)}, u32[]{:S(2)}, u32[]{:S(2)}) %collective-permute-start) | collective-permute-done | bytes 524320 | tf_op jit(solution)/shard_map/ppermute | solution.py:52
  164.8 3.4 %collective-permute-start.2 = (bf16[512,256]{1,0:T(8,128)(2,1)S(1)}, bf16[512,256]{1,0:T(8,128)(2,1)S(1)}, u32[]{:S(2)}, u32[]{:S(2)}) collective-permute-start(bf16[512,256]{1,0:T(8,128)(2,1)S(1)} %slice.10), channel_id=1, source_target_pairs={{0,1},{1,2},{2,3},{3,0},{4,5},{5,6},{6,7},{7,4},{8,9},{9,10},{10,1... | collective-permute-start | bytes 786440 | tf_op jit(solution)/shard_map/ppermute | solution.py:56
  168.3 2.4 %collective-permute-start.3 = (bf16[512,256]{1,0:T(8,128)(2,1)S(1)}, bf16[512,256]{1,0:T(8,128)(2,1)S(1)}, u32[]{:S(2)}, u32[]{:S(2)}) collective-permute-start(bf16[512,256]{1,0:T(8,128)(2,1)S(1)} %slice.11), channel_id=1, source_target_pairs={{0,3},{1,0},{2,1},{3,2},{4,7},{5,4},{6,5},{7,6},{8,11},{9,8},{10,9... | collective-permute-start | bytes 786440 | tf_op jit(solution)/shard_map/ppermute | solution.py:57
  170.8 2.3 %collective-permute-done.2 = bf16[512,256]{1,0:T(8,128)(2,1)S(1)} collective-permute-done((bf16[512,256]{1,0:T(8,128)(2,1)S(1)}, bf16[512,256]{1,0:T(8,128)(2,1)S(1)}, u32[]{:S(2)}, u32[]{:S(2)}) %collective-permute-start.2) | collective-permute-done | bytes 262176 | tf_op jit(solution)/shard_map/ppermute | solution.py:56
  173.1 3.5 %collective-permute-done.3 = bf16[512,256]{1,0:T(8,128)(2,1)S(1)} collective-permute-done((bf16[512,256]{1,0:T(8,128)(2,1)S(1)}, bf16[512,256]{1,0:T(8,128)(2,1)S(1)}, u32[]{:S(2)}, u32[]{:S(2)}) %collective-permute-start.3) | collective-permute-done | bytes 262176 | tf_op jit(solution)/shard_map/ppermute | solution.py:57
  177.0 0.6 copy.27
  178.2 0.6 fusion
  178.8 5.5 %fusion.17 = f32[256,896]{1,0:T(8,128)S(1)} fusion(bf16[4096,256]{1,0:T(8,128)(2,1)S(1)} %fusion, bf16[4096,896]{1,0:T(8,128)(2,1)} %all-gather.2.cloned.1.call-done), kind=kOutput, calls=%fused_computation.36 | convolution fusion | flops 1879048192 | bytes 10354688 | tf_op jit(solution)/shard_map/fk,fo->ko/dot_general | solution.py:90
  184.3 0.6 fusion.1
  185.1 12.3 %psum.7 = f32[1,1,8,256]{3,2,1,0:T(8,128)S(1)} all-reduce(f32[1,1,8,256]{3,2,1,0:T(8,128)S(1)} %convolution_bitcast_fusion), channel_id=1, replica_groups=mesh['fsdp'=32,'dp'=4,'tensor'=4] {'dp'}, use_global_device_ids=true, to_apply=%region_3.4 | all-reduce | flops 2048 | bytes 16384 | tf_op jit(solution)/shard_map/psum | solution.py:100
  197.5 13.5 %all_gather.15 = f32[4,1,8,256]{3,2,1,0:T(8,128)S(1)} all-gather(f32[1,1,8,256]{3,2,1,0:T(8,128)S(1)} %psum.7), channel_id=1, replica_groups=mesh['fsdp'=32,'dp'=4,'tensor'=4] {'tensor'}, dimensions={0}, use_global_device_ids=true | all-gather | bytes 40960 | tf_op jit(solution)/shard_map/all_gather | solution.py:16
  (31 shorter events, 2.4 us)
Async XLA Ops:
  7.2 177.8 %copy-start = (bf16[1,896,256]{2,1,0:T(8,128)(2,1)S(1)}, bf16[1,896,256]{2,1,0:T(8,128)(2,1)}, u32[]{:S(2)}) copy-start(bf16[1,896,256]{2,1,0:T(8,128)(2,1)} %param.17) | copy-start | bytes 1376260
  7.2 42.2 %reduce-scatter.2.cloned.1.call-start = ((), (), s32[]{:S(2)}) async-start(), calls=%async_computation.4 | async-start | bytes 1146880 | tf_op jit(solution)/shard_map/reduce_scatter | solution.py:23
  7.9 59.2 %copy-start.2 = (s32[1,256]{1,0:T(1,128)S(1)}, s32[1,256]{1,0:T(1,128)}, u32[]{:S(2)}) copy-start(s32[1,256]{1,0:T(1,128)} %param.15) | copy-start | bytes 3076
  7.9 69.0 %copy-start.1 = (bf16[8,64128]{1,0:T(8,128)(2,1)S(1)}, bf16[8,64128]{1,0:T(8,128)(2,1)}, u32[]{:S(2)}) copy-start(bf16[8,64128]{1,0:T(8,128)(2,1)} %param.14) | copy-start | bytes 3078148
  7.9 170.9 %all-gather.2.cloned.1.call-start = ((), (), s32[]{:S(2)}) async-start(), calls=%async_computation.5 | async-start | bytes 7569408 | tf_op jit(solution)/shard_map/all_gather | solution.py:85
  67.8 19.8 %all-to-all-start = ((s32[32,1,256]{2,1,0:T(1,128)}), s32[32,1,256]{2,1,0:T(1,128)S(1)}, u32[]{:S(2)}, u32[]{:S(2)}) async-start(s32[32,1,256]{2,1,0:T(1,128)} %broadcast_in_dim.27), calls=%async_computation.1 | async-start | bytes 65536 | tf_op jit(solution)/shard_map/all_to_all | solution.py:63
  87.6 70.5 %copy-start.3 = (s32[1,256]{1,0:T(1,128)S(1)}, s32[1,256]{1,0:T(1,128)}, u32[]{:S(2)}) copy-start(s32[1,256]{1,0:T(1,128)} %param.16) | copy-start | bytes 3076
  152.2 12.6 %collective-permute-start = (bf16[1024,256]{1,0:T(8,128)(2,1)S(1)}, bf16[1024,256]{1,0:T(8,128)(2,1)S(1)}, u32[]{:S(2)}, u32[]{:S(2)}) collective-permute-start(bf16[1024,256]{1,0:T(8,128)(2,1)S(1)} %all_gather.12), channel_id=1, source_target_pairs={{0,1},{1,2},{2,3},{3,0},{4,5},{5,6},{6,7},{7,4},{8,9},{9,10},{10,1... | collective-permute-start | bytes 1572872 | tf_op jit(solution)/shard_map/ppermute | solution.py:52
  155.5 12.7 %collective-permute-start.1 = (bf16[1024,256]{1,0:T(8,128)(2,1)S(1)}, bf16[1024,256]{1,0:T(8,128)(2,1)S(1)}, u32[]{:S(2)}, u32[]{:S(2)}) collective-permute-start(bf16[1024,256]{1,0:T(8,128)(2,1)S(1)} %all_gather.12), channel_id=1, source_target_pairs={{0,3},{1,0},{2,1},{3,2},{4,7},{5,4},{6,5},{7,6},{8,11},{9,8},{10,9... | collective-permute-start | bytes 1572872 | tf_op jit(solution)/shard_map/ppermute | solution.py:53
  164.8 8.3 %collective-permute-start.2 = (bf16[512,256]{1,0:T(8,128)(2,1)S(1)}, bf16[512,256]{1,0:T(8,128)(2,1)S(1)}, u32[]{:S(2)}, u32[]{:S(2)}) collective-permute-start(bf16[512,256]{1,0:T(8,128)(2,1)S(1)} %slice.10), channel_id=1, source_target_pairs={{0,1},{1,2},{2,3},{3,0},{4,5},{5,6},{6,7},{7,4},{8,9},{9,10},{10,1... | collective-permute-start | bytes 786440 | tf_op jit(solution)/shard_map/ppermute | solution.py:56
  168.3 8.3 %collective-permute-start.3 = (bf16[512,256]{1,0:T(8,128)(2,1)S(1)}, bf16[512,256]{1,0:T(8,128)(2,1)S(1)}, u32[]{:S(2)}, u32[]{:S(2)}) collective-permute-start(bf16[512,256]{1,0:T(8,128)(2,1)S(1)} %slice.11), channel_id=1, source_target_pairs={{0,3},{1,0},{2,1},{3,2},{4,7},{5,4},{6,5},{7,6},{8,11},{9,8},{10,9... | collective-permute-start | bytes 786440 | tf_op jit(solution)/shard_map/ppermute | solution.py:57
Sparse Core Ops, SparseCore 0:
  10.8 38.5 reduce-scatter.1
  67.3 73.2 all-gather.1
